TPU v7x, 128 devices: a whole 4x4x4 slice. The times are simulated.
128 devices in a mesh: row: 8 (over x, core), col: 16 (over z, y).
Axes of the slice: x: 4, y: 4, z: 4, core: 2. Of those that a mesh axis runs over, the one named last changes fastest.
Arguments:
- right_sides: bfloat16 [32768, 12288], P('row', 'col'), may hold values from -6 to 6
- factor_panels: bfloat16 [32768, 1024], P(('row', 'col')), may hold values from -0.1875 to 0.1875
- inverse_blocks: float32 [4, 256, 256], replicated, may hold values from -1 to 1, as said below
Outputs:
- solved_sides: float32 [32768, 12288], P('row', 'col')
Inputs may be any that keep to these rules, and one draw needn't show every extreme that they name: `inverse_blocks`: each block is unit lower triangular.
All inputs are finite; a program needn't handle non-finite values.
Results may differ from a plain program's by a relative error of at most 0.003.
Values may be sent and summed in bfloat16 or wider, within the bound.
No kernel may reach another device: no remote copies, remote signals or barrier semaphores. Data moves between devices by JAX's collectives and lax.ppermute only.
A program may use at most 192 MiB of HBM per device.

v0:
```python
import jax
import jax.numpy as jnp
from jax import lax
from jax.sharding import PartitionSpec as P


def from_root(value, axis, root):
    mine = lax.axis_index(axis) == root
    return lax.psum(jnp.where(mine, value, jnp.zeros_like(value)), axis)


def publish(solved, panel_num):
    return from_root(solved.astype(jnp.bfloat16), "row", panel_num)


def per_device(right_sides, factor_panels, inverse_blocks):
    panel_count = inverse_blocks.shape[0]
    panel_width = inverse_blocks.shape[1]
    row_index = lax.axis_index("row")
    current = right_sides.astype(jnp.float32)
    for panel_num in range(panel_count):
        leading = current[:panel_width]
        solved = jnp.dot(inverse_blocks[panel_num], leading, precision=lax.Precision.HIGHEST)
        shared = publish(solved, panel_num)
        columns = factor_panels[:, panel_num * panel_width : (panel_num + 1) * panel_width]
        update = jnp.dot(
            lax.all_gather(columns, "col", axis=0, tiled=True),
            shared,
            preferred_element_type=jnp.float32,
        )
        updated_first = jnp.where(row_index > panel_num, leading - update[:panel_width], leading)
        new_first = jnp.where(row_index == panel_num, solved, updated_first)
        current = jnp.concatenate([new_first, current[panel_width:] - update[panel_width:]], 0)
    return current


def solution(mesh):
    placed = (P("row", "col"), P(("row", "col"), None), P())
    return jax.shard_map(
        per_device, mesh=mesh, in_specs=placed, out_specs=P("row", "col"), check_vma=False
    )
```

profile of v0, /device:TPU:0, one launch (start us, length us, event | category | flops | bytes accessed | tf_op | source)
XLA Modules:
  0.0 335.0 jit_solution(2568119471155261356)
XLA Ops:
  7.4 2.3 convert_select_fusion.3
  9.8 1.9 fusion.14
  11.7 0.5 all-gather.7.cloned.1.call-update
  12.3 8.6 %convert_element_type.15 = f32[4096,768]{1,0:T(8,128)} convert(bf16[4096,768]{1,0:T(8,128)(2,1)} %param.3) | non-fusion elementwise | flops 3145728 | bytes 18874368 | tf_op jit(solution)/shard_map/convert_element_type | solution.py:20
  20.9 53.2 %all-reduce.5.cloned.1.call-done = bf16[256,768]{1,0:T(8,128)(2,1)} async-done(((bf16[256,768]{1,0:T(8,128)(2,1)}), bf16[256,768]{1,0:T(8,128)(2,1)}) %all-reduce.5.cloned.1.call-update) | async-done | bytes 393232 | tf_op jit(solution)/shard_map/psum | solution.py:9
  74.1 3.4 %convolution_bitcast_fusion.3 = f32[4096,768]{1,0:T(8,128)S(1)} fusion(bf16[4096,256]{1,0:T(8,128)(2,1)} %all-gather.5.cloned.1.call-done, bf16[256,768]{1,0:T(8,128)(2,1)} %all-reduce.5.cloned.1.call-done), kind=kOutput, calls=%fused_computation.8 | convolution fusion | flops 1610612736 | bytes 15073280 | tf_op jit(solution)/shard_map/dot_general | solution.py:26
  77.5 4.5 %copy-done = f32[4096,768]{1,0:T(8,128)} copy-done((f32[4096,768]{1,0:T(8,128)}, f32[4096,768]{1,0:T(8,128)S(1)}, u32[]{:S(2)}) %copy-start) | copy-done | bytes 12582936
  82.0 1.3 fusion
  83.3 1.6 convert_select_fusion.2
  85.6 20.7 %all-gather.7.cloned.1.call-done = bf16[4096,256]{1,0:T(8,128)(2,1)} async-done(((bf16[256,256]{1,0:T(8,128)(2,1)}), bf16[4096,256]{1,0:T(8,128)(2,1)}) %all-gather.7.cloned.1.call-update) | async-done | bytes 2097168 | tf_op jit(solution)/shard_map/all_gather | solution.py:27
  106.3 38.7 %all-reduce.7.cloned.1.call-done = bf16[256,768]{1,0:T(8,128)(2,1)} async-done(((bf16[256,768]{1,0:T(8,128)(2,1)}), bf16[256,768]{1,0:T(8,128)(2,1)}) %all-reduce.7.cloned.1.call-update) | async-done | bytes 393232 | tf_op jit(solution)/shard_map/psum | solution.py:9
  145.0 3.4 %convolution_bitcast_fusion.2 = f32[4096,768]{1,0:T(8,128)S(1)} fusion(bf16[4096,256]{1,0:T(8,128)(2,1)} %all-gather.7.cloned.1.call-done, bf16[256,768]{1,0:T(8,128)(2,1)} %all-reduce.7.cloned.1.call-done), kind=kOutput, calls=%fused_computation.7 | convolution fusion | flops 1610612736 | bytes 15073280 | tf_op jit(solution)/shard_map/dot_general | solution.py:26
  148.5 4.5 %copy-done.1 = f32[4096,768]{1,0:T(8,128)} copy-done((f32[4096,768]{1,0:T(8,128)}, f32[4096,768]{1,0:T(8,128)S(1)}, u32[]{:S(2)}) %copy-start.1) | copy-done | bytes 12582936
  153.1 1.6 convert_select_fusion.1
  154.8 0.7 all-gather.11.cloned.1.call-update
  155.8 59.4 %all-reduce.9.cloned.1.call-done = bf16[256,768]{1,0:T(8,128)(2,1)} async-done(((bf16[256,768]{1,0:T(8,128)(2,1)}), bf16[256,768]{1,0:T(8,128)(2,1)}) %all-reduce.9.cloned.1.call-update) | async-done | bytes 393232 | tf_op jit(solution)/shard_map/psum | solution.py:9
  215.2 3.4 %convolution_bitcast_fusion.1 = f32[4096,768]{1,0:T(8,128)S(1)} fusion(bf16[4096,256]{1,0:T(8,128)(2,1)} %all-gather.9.cloned.1.call-done, bf16[256,768]{1,0:T(8,128)(2,1)} %all-reduce.9.cloned.1.call-done), kind=kOutput, calls=%fused_computation.6 | convolution fusion | flops 1610612736 | bytes 15073280 | tf_op jit(solution)/shard_map/dot_general | solution.py:26
  218.6 4.6 %copy-done.2 = f32[4096,768]{1,0:T(8,128)} copy-done((f32[4096,768]{1,0:T(8,128)}, f32[4096,768]{1,0:T(8,128)S(1)}, u32[]{:S(2)}) %copy-start.2) | copy-done | bytes 12582936
  223.3 1.6 convert_select_fusion
  225.0 59.6 %all-reduce.11.cloned.1.call-done = bf16[256,768]{1,0:T(8,128)(2,1)} async-done(((bf16[256,768]{1,0:T(8,128)(2,1)}), bf16[256,768]{1,0:T(8,128)(2,1)}) %all-reduce.11.cloned.1.call-update) | async-done | bytes 393232 | tf_op jit(solution)/shard_map/psum | solution.py:9
  284.6 7.9 %convolution_bitcast_fusion = f32[4096,768]{1,0:T(8,128)} fusion(bf16[4096,256]{1,0:T(8,128)(2,1)} %all-gather.11.cloned.1.call-done, bf16[256,768]{1,0:T(8,128)(2,1)} %all-reduce.11.cloned.1.call-done), kind=kOutput, calls=%fused_computation.5 | convolution fusion | flops 1610612736 | bytes 15073280 | tf_op jit(solution)/shard_map/dot_general | solution.py:26
  292.5 24.0 %slice_subtract_fusion = f32[3840,768]{1,0:T(8,128)} fusion(f32[4096,768]{1,0:T(8,128)} %convolution_bitcast_fusion, f32[4096,768]{1,0:T(8,128)} %copy-done.2, f32[4096,768]{1,0:T(8,128)} %copy-done.1, f32[4096,768]{1,0:T(8,128)} %copy-done, f32[4096,768]{1,0:T(8,128)} %convert_element_type.15), kind=kLoop, calls=%fused_computation.1 | loop fusion | flops 11796480 | bytes 70778880 | tf_op jit(solution)/shard_map/sub | solution.py:33
  316.5 1.3 fusion.3
  317.7 9.9 %pad_maximum_fusion = f32[4096,768]{1,0:T(8,128)} fusion(f32[3840,768]{1,0:T(8,128)} %slice_subtract_fusion, f32[256,768]{1,0:T(8,128)S(1)} %fusion.3), kind=kLoop, calls=%fused_computation | loop fusion | flops 3145728 | bytes 25165824 | tf_op jit(solution)/shard_map/concatenate | solution.py:33
  (24 shorter events, 1.4 us)
Async XLA Ops:
  7.4 66.7 %all-reduce.5.cloned.1.call-start = ((), (), s32[]{:S(2)}) async-start(), calls=%async_computation | async-start | bytes 786432 | tf_op jit(solution)/shard_map/psum | solution.py:9
  9.7 64.4 %all-gather.5.cloned.1.call-start = ((), (), s32[]{:S(2)}) async-start(), calls=%async_computation.1 | async-start | bytes 2228224 | tf_op jit(solution)/shard_map/all_gather | solution.py:27
  11.7 94.7 %all-gather.7.cloned.1.call-start = ((), (), s32[]{:S(2)}) async-start(), calls=%async_computation.3 | async-start | bytes 2228224 | tf_op jit(solution)/shard_map/all_gather | solution.py:27
  12.3 132.8 %all-reduce.7.cloned.1.call-start = ((), (), s32[]{:S(2)}) async-start(), calls=%async_computation.2 | async-start | bytes 786432 | tf_op jit(solution)/shard_map/psum | solution.py:9
  20.9 62.4 %copy-start.3 = (f32[4,256,256]{2,1,0:T(8,128)S(1)}, f32[4,256,256]{2,1,0:T(8,128)}, u32[]{:S(2)}) copy-start(f32[4,256,256]{2,1,0:T(8,128)} %param.5) | copy-start | bytes 3145732
  77.5 4.5 %copy-start = (f32[4096,768]{1,0:T(8,128)}, f32[4096,768]{1,0:T(8,128)S(1)}, u32[]{:S(2)}) copy-start(f32[4096,768]{1,0:T(8,128)S(1)} %convolution_bitcast_fusion.3) | copy-start | bytes 37748740
  85.0 70.8 %all-gather.9.cloned.1.call-start = ((), (), s32[]{:S(2)}) async-start(), calls=%async_computation.5 | async-start | bytes 2228224 | tf_op jit(solution)/shard_map/all_gather | solution.py:27
  85.6 129.6 %all-reduce.9.cloned.1.call-start = ((), (), s32[]{:S(2)}) async-start(), calls=%async_computation.4 | async-start | bytes 786432 | tf_op jit(solution)/shard_map/psum | solution.py:9
  148.5 4.5 %copy-start.1 = (f32[4096,768]{1,0:T(8,128)}, f32[4096,768]{1,0:T(8,128)S(1)}, u32[]{:S(2)}) copy-start(f32[4096,768]{1,0:T(8,128)S(1)} %convolution_bitcast_fusion.2) | copy-start | bytes 37748740
  154.8 70.2 %all-gather.11.cloned.1.call-start = ((), (), s32[]{:S(2)}) async-start(), calls=%async_computation.7 | async-start | bytes 2228224 | tf_op jit(solution)/shard_map/all_gather | solution.py:27
  155.5 129.1 %all-reduce.11.cloned.1.call-start = ((), (), s32[]{:S(2)}) async-start(), calls=%async_computation.6 | async-start | bytes 786432 | tf_op jit(solution)/shard_map/psum | solution.py:9
  218.6 4.6 %copy-start.2 = (f32[4096,768]{1,0:T(8,128)}, f32[4096,768]{1,0:T(8,128)S(1)}, u32[]{:S(2)}) copy-start(f32[4096,768]{1,0:T(8,128)S(1)} %convolution_bitcast_fusion.1) | copy-start | bytes 37748740
Sparse Core Ops, SparseCore 0:
  10.5 63.5 all-reduce.4
  85.1 59.8 all-reduce.6
  154.9 60.2 all-reduce.8
  225.1 59.4 all-reduce.10
Sparse Core Ops, SparseCore 1:
  12.3 47.6 all-gather.4
  62.0 44.3 all-gather.6
  108.4 44.3 all-gather.8
  157.7 44.2 all-gather.10
where the time goes:
time: 335 us
  waiting for transfers between devices  233 us (70%)
  other arithmetic  45.3 us (14%)
  matrix products  25.3 us (8%)
  local copies, waits for them, and re-layouts  15.5 us (5%)
  between operations  15 us (4%)
    psum x4, waiting for transfers between devices, from_root(): return lax.psum(jnp.where(mine, value, jnp.zeros_like(value)), axis)  211 us
    sub x1, other arithmetic, per_device(): current[panel_width:] - update[panel_width:]  24 us
    all_gather x4, waiting for transfers between devices, per_device(): lax.all_gather(columns, 'col', axis=0, tiled=True)  20.8 us
    dot_general x4, matrix products, per_device(): jnp.dot(lax.all_gather(columns, 'col', axis=0, tiled=True), shared, prefe...  18.2 us
    unnamed x8, local copies, waits for them, and re-layouts  13.6 us
    concatenate x1, other arithmetic, per_device(): jnp.concatenate([new_first, current[panel_width:] - update[panel_width:]]...  9.94 us
    convert_element_type x1, other arithmetic, per_device(): current = right_sides.astype(jnp.float32)  8.55 us
    dot_general x4, matrix products, per_device(): jnp.dot(inverse_blocks[panel_num], leading, precision=lax.Precision.HIGHEST)  7.15 us
  transfers between devices with their start and end apart: 8, of which 5 were waited for; matrix products, arithmetic and copies ran while one was open for 8% of the time, Pallas kernels for 0%

commit v1 on v0

v1 whole, which is shorter than its diff:
```python
import jax
import jax.numpy as jnp
from jax import lax
from jax.experimental import pallas as pl
from jax.experimental.pallas import tpu as pltpu
from jax.sharding import PartitionSpec as P


BF = jnp.bfloat16
F32 = jnp.float32
SIDE = 4
RING = 4
STEPS = (1, 3, 2)
BOTH = ("row", "col")


def y_to(c, d):
    return (c // SIDE) * SIDE + (c % SIDE + d) % SIDE


def z_to(c, d):
    return (c // SIDE + d) % SIDE * SIDE + c % SIDE


def plane_perm(d, turned):
    return [
        (r * 16 + c, r * 16 + (z_to if r % 2 != turned else y_to)(c, d))
        for r in range(8)
        for c in range(16)
    ]


def x_perm(move):
    return [(x * 2 + k, move(x) * 2 + k) for x in range(SIDE) for k in range(2)]


SWAP = [(r, r ^ 1) for r in range(8)]


def dot(a, b):
    return jnp.dot(a, b, preferred_element_type=F32)


def main_kernel(*refs):
    own = refs[0]
    near, turned, far = refs[1:4], refs[4:7], refs[7:10]
    shared_ref, top_ref, rhs_ref, out_ref, obuf, osem = refs[10:]
    size = own.shape[0]
    row, col = lax.axis_index("row"), lax.axis_index("col")
    z, y = col // SIDE, col % SIDE
    core = lax.rem(row, 2)

    def emit(slot, factor, along, across):
        dy = jnp.where(core == 0, along, across)
        dz = jnp.where(core == 0, across, along)
        if slot >= RING:
            pltpu.make_async_copy(obuf.at[0], obuf.at[0], osem.at[slot % RING]).wait()
        slot = slot % RING
        block = lax.rem(z + SIDE - dz, SIDE) * SIDE + lax.rem(y + SIDE - dy, SIDE)
        begin = pl.multiple_of(block * size, size)
        obuf[slot] = rhs_ref[pl.ds(begin, size), :].astype(F32) - dot(factor, shared_ref[...])

        @pl.when(jnp.logical_and(block == 0, row < 4))
        def _():
            obuf[slot] = top_ref[...]

        pltpu.make_async_copy(
            obuf.at[slot], out_ref.at[pl.ds(begin, size), :], osem.at[slot]
        ).start()

    emit(0, own[...], 0, 0)
    for i, d in enumerate(STEPS):
        emit(1 + i, near[i][...], d, 0)
        emit(4 + i, turned[i][...], 0, d)
    for i, e in enumerate(STEPS):
        for j, d in enumerate(STEPS):
            emit(7 + 3 * i + j, far[i][j * size : (j + 1) * size, :], d, e)
    for slot in range(RING):
        pltpu.make_async_copy(obuf.at[slot], obuf.at[slot], osem.at[slot]).wait()


def main_call(own, near, turned, far, shared, top, rhs):
    rows, width = rhs.shape
    size, depth = own.shape
    vmem = pl.BlockSpec(memory_space=pltpu.VMEM)
    args = [own, *near, *turned, *far, shared, top, rhs]
    return pl.pallas_call(
        main_kernel,
        out_shape=jax.ShapeDtypeStruct((rows, width), F32),
        in_specs=[vmem] * len(args),
        out_specs=pl.BlockSpec(memory_space=pl.ANY),
        scratch_shapes=[
            pltpu.VMEM((RING, size, width), F32),
            pltpu.SemaphoreType.DMA((RING,)),
        ],
        compiler_params=pltpu.CompilerParams(vmem_limit_bytes=24 << 20),
        cost_estimate=pl.CostEstimate(
            flops=2 * rows * depth * width, bytes_accessed=rows * width * 4, transcendentals=0
        ),
        name="update",
    )(*args)


def split(value):
    high = value.astype(BF)
    return high, (value - high.astype(F32)).astype(BF)


def solve_kernel(*refs):
    own_rows, other_rows = refs[0:2], refs[2:4]
    own_low, other_low = refs[4:8], refs[8:12]
    inverse_ref, shared_ref, top_ref, low = refs[12:]
    row = lax.axis_index("row")
    x, core = row // 2, lax.rem(row, 2)
    size = inverse_ref.shape[1]
    quarter = size // SIDE
    for i, d in enumerate((0, *STEPS)):
        place = pl.multiple_of(lax.rem(x + SIDE - d, SIDE) * quarter, quarter)
        mine, theirs = own_low[i][...], other_low[i][...]
        low[0, pl.ds(place, quarter), :] = jnp.where(core == 0, mine, theirs)
        low[1, pl.ds(place, quarter), :] = jnp.where(core == 0, theirs, mine)
    outer = jnp.logical_or(x == 0, x == 3)
    for k in range(inverse_ref.shape[0]):
        here = outer if k < 2 else jnp.logical_not(outer)
        mine = jnp.where(here, own_rows[0][...], own_rows[1][...])
        theirs = jnp.where(here, other_rows[0][...], other_rows[1][...])
        current = jnp.where(core == k % 2, mine, theirs).astype(F32)
        if k:
            begin = 0 if k < 2 else size
            current -= dot(low[k % 2, :, begin : begin + k * size], shared_ref[: k * size, :])
        ih, il = split(inverse_ref[k])
        ch, cl = split(current)
        solved = dot(ih, ch) + (dot(ih, cl) + dot(il, ch))
        shared_ref[k * size : (k + 1) * size, :] = solved.astype(BF)

        @pl.when(row == k)
        def _():
            top_ref[...] = solved


def solve_call(own_rows, other_rows, own_low, other_low, inverse):
    panels, size, _ = inverse.shape
    width = own_rows[0].shape[1]
    vmem = pl.BlockSpec(memory_space=pltpu.VMEM)
    args = [*own_rows, *other_rows, *own_low, *other_low, inverse]
    return pl.pallas_call(
        solve_kernel,
        out_shape=(
            jax.ShapeDtypeStruct((panels * size, width), BF),
            jax.ShapeDtypeStruct((size, width), F32),
        ),
        in_specs=[vmem] * len(args),
        out_specs=(vmem, vmem),
        scratch_shapes=[pltpu.VMEM((2, size, 4 * size), BF)],
        compiler_params=pltpu.CompilerParams(vmem_limit_bytes=12 << 20),
        cost_estimate=pl.CostEstimate(
            flops=2 * 18 * size * size * width, bytes_accessed=6 << 20, transcendentals=0
        ),
        name="solve",
    )(*args)


def pick(index, at0, at1, at2, at3):
    return jnp.where(
        index == 0, at0, jnp.where(index == 1, at1, jnp.where(index == 2, at2, at3))
    )


def per_device(right_sides, factor_panels, inverse_blocks):
    size = inverse_blocks.shape[1]
    quarter = size // SIDE
    row = lax.axis_index("row")
    col = lax.axis_index("col")
    x, core = row // 2, row % 2
    z, y = col // SIDE, col % SIDE

    def along(value, d):
        return lax.ppermute(value, BOTH, plane_perm(d, 0))

    def across(value, d):
        return lax.ppermute(value, BOTH, plane_perm(d, 1))

    def over_x(value, move):
        return lax.ppermute(value, "row", x_perm(move))

    def swap(value):
        return lax.ppermute(value, "row", SWAP)

    def quarter_of(chip):
        return lax.dynamic_slice(factor_panels, (quarter * chip, 0), (quarter, 3 * size))

    got = {0: quarter_of(x)}
    for d in STEPS:
        got[d] = over_x(quarter_of((x + d) % SIDE), lambda s: (s + d) % SIDE)
    first = pick(x, got[0], got[1], got[2], got[3])
    second = pick(x, got[3], got[0], got[1], got[2])
    low = jnp.concatenate([first[:, :size], second], axis=1)

    near = [along(factor_panels, d) for d in STEPS]
    lead = right_sides[:size]
    passed = over_x(lead, lambda s: 3 - s)

    spot = jnp.where(core == 0, z, y)
    parts = {d: across(low, d) for d in STEPS}
    low = pick(spot, low, parts[1], parts[2], parts[3])
    turned = [across(factor_panels, d) for d in STEPS]
    spot = jnp.where(core == 0, y, z)
    parts = {d: along(low, d) for d in STEPS}
    low = pick(spot, low, parts[1], parts[2], parts[3])

    mine = jnp.where(x < 2, lead, passed)
    theirs = over_x(mine, lambda s: s ^ 1)
    own_rows = [mine, theirs]
    other_rows = [swap(mine), swap(theirs)]

    far = [across(jnp.concatenate(near, 0), e) for e in STEPS]

    own_low = [low] + [over_x(low, lambda s: (s + d) % SIDE) for d in STEPS]
    other_low = [swap(v) for v in own_low]

    shared, top = solve_call(own_rows, other_rows, own_low, other_low, inverse_blocks)
    return main_call(factor_panels, near, turned, far, shared, top, right_sides)


def solution(mesh):
    placed = (P("row", "col"), P(BOTH, None), P())

    return jax.shard_map(
        per_device, mesh=mesh, in_specs=placed, out_specs=P("row", "col"), check_vma=False
    )
```

time: 335 us -> 134 us (0.40)
  waiting for transfers between devices: 233 us -> 46.5 us
  starting transfers between devices: 0.48 us -> 52.9 us
  other arithmetic: 45.3 us -> 3.15 us
  matrix products: 25.3 us -> 0 us
  Pallas kernels: 0 us -> 20.3 us
  between operations: 15 us -> 0.31 us
  local copies, waits for them, and re-layouts: 15.5 us -> 9.11 us
    psum x4 -> x0, waiting for transfers between devices: 211 us -> none  [from_root(): return lax.psum(jnp.where(mine, value, jnp.zeros_like(value)), axis)]
    ppermute x0 -> x29, starting transfers between devices: none -> 52.9 us  [the longest x8 29.9 us: over_x(): return lax.ppermute(value, 'row', x_perm(move))]
    ppermute x0 -> x29, waiting for transfers between devices: none -> 46.5 us  [the longest x9 23.7 us: across(): return lax.ppermute(value, BOTH, plane_perm(d, 1))]
    dot_general x8 -> x0, matrix products: 25.3 us -> none  [the longest x4 18.2 us: per_device(): jnp.dot(lax.all_gather(columns, 'col', axis=0, tiled=True), shared, prefe...]
    sub x1 -> x0, other arithmetic: 24 us -> none  [per_device(): current[panel_width:] - update[panel_width:]]
    all_gather x4 -> x0, waiting for transfers between devices: 20.8 us -> none  [per_device(): lax.all_gather(columns, 'col', axis=0, tiled=True)]
    pallas_call x0 -> x2, Pallas kernels: none -> 20.3 us  [the longest x1 15.7 us: main_call(): pl.pallas_call(main_kernel, out_shape=jax.ShapeDtypeStruct((rows, width),...]
    concatenate x1, other arithmetic: 9.94 us -> 0.01 us  [per_device(): low = jnp.concatenate([first[:, :size], second], axis=1)]
  transfers between devices with their start and end apart: 8 -> 29, of which waited for: 5 -> 13; matrix products, arithmetic and copies ran while one was open for 8% -> 5% of each run, Pallas kernels for 0% -> 4%
where the time goes in v1:
time: 134 us; the launch traced here: 132 us
  starting transfers between devices  52.9 us (39%)
  waiting for transfers between devices  46.5 us (35%)
  Pallas kernels  20.3 us (15%)
  local copies, waits for them, and re-layouts  9.11 us (7%)
  other arithmetic  3.15 us (2%)
    ppermute x8, starting transfers between devices, over_x(): return lax.ppermute(value, 'row', x_perm(move))  29.9 us
    ppermute x9, waiting for transfers between devices, across(): return lax.ppermute(value, BOTH, plane_perm(d, 1))  23.7 us
    ppermute x8, waiting for transfers between devices, over_x(): return lax.ppermute(value, 'row', x_perm(move))  16.8 us
    pallas_call x1, Pallas kernels, main_call(): pl.pallas_call(main_kernel, out_shape=jax.ShapeDtypeStruct((rows, width),...  15.7 us
    ppermute x9, starting transfers between devices, across(): return lax.ppermute(value, BOTH, plane_perm(d, 1))  13.1 us
    ppermute x6, starting transfers between devices, along(): return lax.ppermute(value, BOTH, plane_perm(d, 0))  8.95 us
    pallas_call x1, Pallas kernels, solve_call(): pl.pallas_call(solve_kernel, out_shape=(jax.ShapeDtypeStruct((panels * si...  4.64 us
    unnamed x14, local copies, waits for them, and re-layouts  4.45 us
  transfers between devices with their start and end apart: 29, of which 13 were waited for; matrix products, arithmetic and copies ran while one was open for 5% of the time, Pallas kernels for 4%

profile of v1, /device:TPU:0, one launch (start us, length us, event | category | flops | bytes accessed | tf_op | source)
XLA Modules:
  0.0 132.3 jit_solution(15468120297717135679)
XLA Ops:
  1.0 3.2 %collective-permute-start.14 = (bf16[64,768]{1,0:T(8,128)(2,1)S(1)}, bf16[64,768]{1,0:T(8,128)(2,1)S(1)}, u32[]{:S(2)}, u32[]{:S(2)}) collective-permute-start(bf16[64,768]{1,0:T(8,128)(2,1)S(1)} %get-tuple-element.9), channel_id=1, source_target_pairs={{0,64},{16,80},{32,96},{48,112},{64,0},{80,16},{96,32},{112,48},{1... | collective-permute-start | bytes 294920 | tf_op jit(solution)/shard_map/ppermute | solution.py:184
  4.8 2.6 %collective-permute-start.15 = (bf16[64,768]{1,0:T(8,128)(2,1)S(1)}, bf16[64,768]{1,0:T(8,128)(2,1)S(1)}, u32[]{:S(2)}, u32[]{:S(2)}) collective-permute-start(bf16[64,768]{1,0:T(8,128)(2,1)S(1)} %get-tuple-element.11), channel_id=1, source_target_pairs={{0,96},{16,112},{32,0},{48,16},{64,32},{80,48},{96,64},{112,80},{1... | collective-permute-start | bytes 294920 | tf_op jit(solution)/shard_map/ppermute | solution.py:184
  7.5 2.6 %collective-permute-done.13 = bf16[64,768]{1,0:T(8,128)(2,1)S(1)} collective-permute-done((bf16[64,768]{1,0:T(8,128)(2,1)S(1)}, bf16[64,768]{1,0:T(8,128)(2,1)S(1)}, u32[]{:S(2)}, u32[]{:S(2)}) %collective-permute-start.13) | collective-permute-done | bytes 98336 | tf_op jit(solution)/shard_map/ppermute | solution.py:184
  11.8 4.1 %collective-permute-start.18 = (bf16[64,1024]{1,0:T(8,128)(2,1)S(1)}, bf16[64,1024]{1,0:T(8,128)(2,1)S(1)}, u32[]{:S(2)}, u32[]{:S(2)}) collective-permute-start(bf16[64,1024]{1,0:T(8,128)(2,1)S(1)} %pad_maximum_fusion), channel_id=1, source_target_pairs={{0,12},{1,13},{2,14},{3,15},{4,0},{5,1},{6,2},{7,3},{8,4},{9,5},{1... | collective-permute-start | bytes 393224 | tf_op jit(solution)/shard_map/ppermute | solution.py:181
  17.2 1.6 %collective-permute-start = (bf16[256,1024]{1,0:T(8,128)(2,1)}, bf16[256,1024]{1,0:T(8,128)(2,1)S(1)}, u32[]{:S(2)}, u32[]{:S(2)}) collective-permute-start(bf16[256,1024]{1,0:T(8,128)(2,1)} %refs_0_.1), channel_id=1, source_target_pairs={{0,1},{1,2},{2,3},{3,0},{4,5},{5,6},{6,7},{7,4},{8,9},{9,10},{10,1... | collective-permute-start | bytes 1572872 | tf_op jit(solution)/shard_map/ppermute | solution.py:178
  19.9 4.0 %collective-permute-done.17 = bf16[64,1024]{1,0:T(8,128)(2,1)S(1)} collective-permute-done((bf16[64,1024]{1,0:T(8,128)(2,1)S(1)}, bf16[64,1024]{1,0:T(8,128)(2,1)S(1)}, u32[]{:S(2)}, u32[]{:S(2)}) %collective-permute-start.17) | collective-permute-done | bytes 131104 | tf_op jit(solution)/shard_map/ppermute | solution.py:181
  25.0 3.1 %collective-permute-start.21 = (bf16[64,1024]{1,0:T(8,128)(2,1)S(1)}, bf16[64,1024]{1,0:T(8,128)(2,1)S(1)}, u32[]{:S(2)}, u32[]{:S(2)}) collective-permute-start(bf16[64,1024]{1,0:T(8,128)(2,1)S(1)} %select_select_fusion.1), channel_id=1, source_target_pairs={{0,3},{1,0},{2,1},{3,2},{4,7},{5,4},{6,5},{7,6},{8,11},{9,8},{10,9... | collective-permute-start | bytes 393224 | tf_op jit(solution)/shard_map/ppermute | solution.py:178
  32.0 1.6 %collective-permute-start.2 = (bf16[256,1024]{1,0:T(8,128)(2,1)}, bf16[256,1024]{1,0:T(8,128)(2,1)}, u32[]{:S(2)}, u32[]{:S(2)}) collective-permute-start(bf16[256,1024]{1,0:T(8,128)(2,1)} %refs_0_.1), channel_id=1, source_target_pairs={{0,2},{1,3},{2,0},{3,1},{4,6},{5,7},{6,4},{7,5},{8,10},{9,11},{10,... | collective-permute-start | bytes 1572872 | tf_op jit(solution)/shard_map/ppermute | solution.py:178
  33.6 1.8 %slice.6 = bf16[256,768]{1,0:T(8,128)(2,1)} slice(bf16[4096,768]{1,0:T(8,128)(2,1)} %refs_12_.3), slice={[0:256], [0:768]} | slice | bytes 786432 | tf_op jit(solution)/shard_map/slice | solution.py:200
  35.4 3.2 %collective-permute-start.9 = (bf16[256,768]{1,0:T(8,128)(2,1)}, bf16[256,768]{1,0:T(8,128)(2,1)}, u32[]{:S(2)}, u32[]{:S(2)}) collective-permute-start(bf16[256,768]{1,0:T(8,128)(2,1)} %slice.6), channel_id=1, source_target_pairs={{0,96},{16,112},{32,64},{48,80},{64,32},{80,48},{96,0},{112,16},{1... | collective-permute-start | bytes 1179656 | tf_op jit(solution)/shard_map/ppermute | solution.py:184
  38.7 1.3 collective-permute-start.5
  40.9 5.8 %collective-permute-done.9 = bf16[256,768]{1,0:T(8,128)(2,1)} collective-permute-done((bf16[256,768]{1,0:T(8,128)(2,1)}, bf16[256,768]{1,0:T(8,128)(2,1)}, u32[]{:S(2)}, u32[]{:S(2)}) %collective-permute-start.9) | collective-permute-done | bytes 393248 | tf_op jit(solution)/shard_map/ppermute | solution.py:184
  46.8 2.2 %collective-permute-done.1.refs_2_ = bf16[256,1024]{1,0:T(8,128)(2,1)S(1)} collective-permute-done((bf16[256,1024]{1,0:T(8,128)(2,1)}, bf16[256,1024]{1,0:T(8,128)(2,1)S(1)}, u32[]{:S(2)}, u32[]{:S(2)}) %collective-permute-start.1) | collective-permute-done | bytes 524320 | tf_op jit(solution)/shard_map/ppermute | solution.py:178
  49.0 20.1 %collective-permute-start.23 = (bf16[64,1024]{1,0:T(8,128)(2,1)S(1)}, bf16[64,1024]{1,0:T(8,128)(2,1)S(1)}, u32[]{:S(2)}, u32[]{:S(2)}) collective-permute-start(bf16[64,1024]{1,0:T(8,128)(2,1)S(1)} %select_select_fusion.refs_4_), channel_id=1, source_target_pairs={{0,96},{16,112},{32,0},{48,16},{64,32},{80,48},{96,64},{112,80},{1... | collective-permute-start | bytes 393224 | tf_op jit(solution)/shard_map/ppermute | solution.py:184
  69.9 1.9 %constant_dynamic-update-slice_fusion = bf16[768,1024]{1,0:T(8,128)(2,1)} fusion(bf16[768,1024]{1,0:T(8,128)(2,1)} %constant_dynamic-update-slice_fusion.1, bf16[256,1024]{1,0:T(8,128)(2,1)} %collective-permute-done.2.refs_3_), kind=kLoop, calls=%fused_computation.8 | loop fusion | bytes 1048576 | tf_op jit(solution)/shard_map/concatenate | solution.py:216
  71.8 2.4 %collective-permute-start.7 = (bf16[768,1024]{1,0:T(8,128)(2,1)}, bf16[768,1024]{1,0:T(8,128)(2,1)}, u32[]{:S(2)}, u32[]{:S(2)}) collective-permute-start(bf16[768,1024]{1,0:T(8,128)(2,1)} %constant_dynamic-update-slice_fusion), channel_id=1, source_target_pairs={{0,12},{1,13},{2,14},{3,15},{4,0},{5,1},{6,2},{7,3},{8,4},{9,5},{1... | collective-permute-start | bytes 4718600 | tf_op jit(solution)/shard_map/ppermute | solution.py:181
  76.2 1.3 broadcast_select_fusion.refs_0_
  78.0 1.3 collective-permute-done.27.refs_10_
  79.5 1.3 collective-permute-done.26.refs_9_
  81.1 7.8 %collective-permute-done.10.refs_1_ = bf16[256,768]{1,0:T(8,128)(2,1)S(1)} collective-permute-done((bf16[256,768]{1,0:T(8,128)(2,1)S(1)}, bf16[256,768]{1,0:T(8,128)(2,1)S(1)}, u32[]{:S(2)}, u32[]{:S(2)}) %collective-permute-start.10) | collective-permute-done | bytes 393248 | tf_op jit(solution)/shard_map/ppermute | solution.py:184
  88.9 2.4 %collective-permute-start.4 = (bf16[256,1024]{1,0:T(8,128)(2,1)}, bf16[256,1024]{1,0:T(8,128)(2,1)S(1)}, u32[]{:S(2)}, u32[]{:S(2)}) collective-permute-start(bf16[256,1024]{1,0:T(8,128)(2,1)} %refs_0_.1), channel_id=1, source_target_pairs={{0,12},{1,13},{2,14},{3,15},{4,0},{5,1},{6,2},{7,3},{8,4},{9,5},{1... | collective-permute-start | bytes 1572872 | tf_op jit(solution)/shard_map/ppermute | solution.py:181
  94.2 4.6 %solve.1 = (bf16[1024,768]{1,0:T(8,128)(2,1)S(1)}, f32[256,768]{1,0:T(8,128)S(1)}) custom-call(bf16[256,768]{1,0:T(8,128)(2,1)S(1)} %broadcast_select_fusion.refs_0_, bf16[256,768]{1,0:T(8,128)(2,1)S(1)} %collective-permute-done.10.refs_1_, bf16[256,768]{1,0:T(8,128)(2,1)S(1)} %collective-permute-done.11.refs_2_, ...), custom_call_target="tpu_custom_call" | custom-call | flops 1811939328 | bytes 6291456 | tf_op jit(solution)/shard_map/solve/pallas_call | solution.py:146
  98.9 17.3 %collective-permute-done.4.refs_5_ = bf16[256,1024]{1,0:T(8,128)(2,1)S(1)} collective-permute-done((bf16[256,1024]{1,0:T(8,128)(2,1)}, bf16[256,1024]{1,0:T(8,128)(2,1)S(1)}, u32[]{:S(2)}, u32[]{:S(2)}) %collective-permute-start.4) | collective-permute-done | bytes 524320 | tf_op jit(solution)/shard_map/ppermute | solution.py:181
  116.4 15.7 %update.1 = f32[4096,768]{1,0:T(8,128)} custom-call(bf16[256,1024]{1,0:T(8,128)(2,1)} %refs_0_.1, bf16[256,1024]{1,0:T(8,128)(2,1)S(1)} %collective-permute-done.refs_1_, bf16[256,1024]{1,0:T(8,128)(2,1)S(1)} %collective-permute-done.1.refs_2_, bf16[256,1024]{1,0:T(8,128)(2,1)} %collective-permute-done.2.refs_3_, ...), custom_call_target="tpu_custom_call" | custom-call | flops 6442450944 | bytes 12582912 | tf_op jit(solution)/shard_map/update/pallas_call | solution.py:87
  (60 shorter events, 18.7 us)
Async XLA Ops:
  1.0 6.5 %collective-permute-start.14 = (bf16[64,768]{1,0:T(8,128)(2,1)S(1)}, bf16[64,768]{1,0:T(8,128)(2,1)S(1)}, u32[]{:S(2)}, u32[]{:S(2)}) collective-permute-start(bf16[64,768]{1,0:T(8,128)(2,1)S(1)} %get-tuple-element.9), channel_id=1, source_target_pairs={{0,64},{16,80},{32,96},{48,112},{64,0},{80,16},{96,32},{112,48},{1... | collective-permute-start | bytes 294920 | tf_op jit(solution)/shard_map/ppermute | solution.py:184
  4.2 5.8 %collective-permute-start.13 = (bf16[64,768]{1,0:T(8,128)(2,1)S(1)}, bf16[64,768]{1,0:T(8,128)(2,1)S(1)}, u32[]{:S(2)}, u32[]{:S(2)}) collective-permute-start(bf16[64,768]{1,0:T(8,128)(2,1)S(1)} %get-tuple-element.10), channel_id=1, source_target_pairs={{0,32},{16,48},{32,64},{48,80},{64,96},{80,112},{96,0},{112,16},{1... | collective-permute-start | bytes 294920 | tf_op jit(solution)/shard_map/ppermute | solution.py:184
  11.8 8.0 %collective-permute-start.18 = (bf16[64,1024]{1,0:T(8,128)(2,1)S(1)}, bf16[64,1024]{1,0:T(8,128)(2,1)S(1)}, u32[]{:S(2)}, u32[]{:S(2)}) collective-permute-start(bf16[64,1024]{1,0:T(8,128)(2,1)S(1)} %pad_maximum_fusion), channel_id=1, source_target_pairs={{0,12},{1,13},{2,14},{3,15},{4,0},{5,1},{6,2},{7,3},{8,4},{9,5},{1... | collective-permute-start | bytes 393224 | tf_op jit(solution)/shard_map/ppermute | solution.py:181
  15.9 7.9 %collective-permute-start.17 = (bf16[64,1024]{1,0:T(8,128)(2,1)S(1)}, bf16[64,1024]{1,0:T(8,128)(2,1)S(1)}, u32[]{:S(2)}, u32[]{:S(2)}) collective-permute-start(bf16[64,1024]{1,0:T(8,128)(2,1)S(1)} %pad_maximum_fusion), channel_id=1, source_target_pairs={{0,8},{1,9},{2,10},{3,11},{4,12},{5,13},{6,14},{7,15},{8,0},{9,1},... | collective-permute-start | bytes 393224 | tf_op jit(solution)/shard_map/ppermute | solution.py:181
  15.9 9.0 %collective-permute-start.16 = (bf16[64,1024]{1,0:T(8,128)(2,1)S(1)}, bf16[64,1024]{1,0:T(8,128)(2,1)S(1)}, u32[]{:S(2)}, u32[]{:S(2)}) collective-permute-start(bf16[64,1024]{1,0:T(8,128)(2,1)S(1)} %pad_maximum_fusion), channel_id=1, source_target_pairs={{0,4},{1,5},{2,6},{3,7},{4,8},{5,9},{6,10},{7,11},{8,12},{9,13},{1... | collective-permute-start | bytes 393224 | tf_op jit(solution)/shard_map/ppermute | solution.py:181
  17.2 22.8 %collective-permute-start = (bf16[256,1024]{1,0:T(8,128)(2,1)}, bf16[256,1024]{1,0:T(8,128)(2,1)S(1)}, u32[]{:S(2)}, u32[]{:S(2)}) collective-permute-start(bf16[256,1024]{1,0:T(8,128)(2,1)} %refs_0_.1), channel_id=1, source_target_pairs={{0,1},{1,2},{2,3},{3,0},{4,5},{5,6},{6,7},{7,4},{8,9},{9,10},{10,1... | collective-permute-start | bytes 1572872 | tf_op jit(solution)/shard_map/ppermute | solution.py:178
  25.0 7.0 %collective-permute-start.21 = (bf16[64,1024]{1,0:T(8,128)(2,1)S(1)}, bf16[64,1024]{1,0:T(8,128)(2,1)S(1)}, u32[]{:S(2)}, u32[]{:S(2)}) collective-permute-start(bf16[64,1024]{1,0:T(8,128)(2,1)S(1)} %select_select_fusion.1), channel_id=1, source_target_pairs={{0,3},{1,0},{2,1},{3,2},{4,7},{5,4},{6,5},{7,6},{8,11},{9,8},{10,9... | collective-permute-start | bytes 393224 | tf_op jit(solution)/shard_map/ppermute | solution.py:178
  28.1 7.3 %collective-permute-start.20 = (bf16[64,1024]{1,0:T(8,128)(2,1)S(1)}, bf16[64,1024]{1,0:T(8,128)(2,1)S(1)}, u32[]{:S(2)}, u32[]{:S(2)}) collective-permute-start(bf16[64,1024]{1,0:T(8,128)(2,1)S(1)} %select_select_fusion.1), channel_id=1, source_target_pairs={{0,2},{1,3},{2,0},{3,1},{4,6},{5,7},{6,4},{7,5},{8,10},{9,11},{10,... | collective-permute-start | bytes 393224 | tf_op jit(solution)/shard_map/ppermute | solution.py:178
  28.7 20.3 %collective-permute-start.1 = (bf16[256,1024]{1,0:T(8,128)(2,1)}, bf16[256,1024]{1,0:T(8,128)(2,1)S(1)}, u32[]{:S(2)}, u32[]{:S(2)}) collective-permute-start(bf16[256,1024]{1,0:T(8,128)(2,1)} %refs_0_.1), channel_id=1, source_target_pairs={{0,3},{1,0},{2,1},{3,2},{4,7},{5,4},{6,5},{7,6},{8,11},{9,8},{10,9... | collective-permute-start | bytes 1572872 | tf_op jit(solution)/shard_map/ppermute | solution.py:178
  29.8 8.9 %collective-permute-start.19 = (bf16[64,1024]{1,0:T(8,128)(2,1)S(1)}, bf16[64,1024]{1,0:T(8,128)(2,1)}, u32[]{:S(2)}, u32[]{:S(2)}) collective-permute-start(bf16[64,1024]{1,0:T(8,128)(2,1)S(1)} %select_select_fusion.1), channel_id=1, source_target_pairs={{0,1},{1,2},{2,3},{3,0},{4,5},{5,6},{6,7},{7,4},{8,9},{9,10},{10,1... | collective-permute-start | bytes 393224 | tf_op jit(solution)/shard_map/ppermute | solution.py:178
  32.0 37.9 %collective-permute-start.2 = (bf16[256,1024]{1,0:T(8,128)(2,1)}, bf16[256,1024]{1,0:T(8,128)(2,1)}, u32[]{:S(2)}, u32[]{:S(2)}) collective-permute-start(bf16[256,1024]{1,0:T(8,128)(2,1)} %refs_0_.1), channel_id=1, source_target_pairs={{0,2},{1,3},{2,0},{3,1},{4,6},{5,7},{6,4},{7,5},{8,10},{9,11},{10,... | collective-permute-start | bytes 1572872 | tf_op jit(solution)/shard_map/ppermute | solution.py:178
  35.4 11.4 %collective-permute-start.9 = (bf16[256,768]{1,0:T(8,128)(2,1)}, bf16[256,768]{1,0:T(8,128)(2,1)}, u32[]{:S(2)}, u32[]{:S(2)}) collective-permute-start(bf16[256,768]{1,0:T(8,128)(2,1)} %slice.6), channel_id=1, source_target_pairs={{0,96},{16,112},{32,64},{48,80},{64,32},{80,48},{96,0},{112,16},{1... | collective-permute-start | bytes 1179656 | tf_op jit(solution)/shard_map/ppermute | solution.py:184
  38.7 38.9 %collective-permute-start.5 = (bf16[256,1024]{1,0:T(8,128)(2,1)}, bf16[256,1024]{1,0:T(8,128)(2,1)}, u32[]{:S(2)}, u32[]{:S(2)}) collective-permute-start(bf16[256,1024]{1,0:T(8,128)(2,1)} %refs_0_.1), channel_id=1, source_target_pairs={{0,8},{1,9},{2,10},{3,11},{4,12},{5,13},{6,14},{7,15},{8,0},{9,1},... | collective-permute-start | bytes 1572872 | tf_op jit(solution)/shard_map/ppermute | solution.py:181
  40.0 31.8 %collective-permute-start.25 = (bf16[64,1024]{1,0:T(8,128)(2,1)S(1)}, bf16[64,1024]{1,0:T(8,128)(2,1)S(1)}, u32[]{:S(2)}, u32[]{:S(2)}) collective-permute-start(bf16[64,1024]{1,0:T(8,128)(2,1)S(1)} %select_select_fusion.refs_4_), channel_id=1, source_target_pairs={{0,16},{16,0},{32,48},{48,32},{64,80},{80,64},{96,112},{112,96},{1... | collective-permute-start | bytes 393224 | tf_op jit(solution)/shard_map/ppermute | solution.py:187
  46.8 25.0 %collective-permute-start.24 = (bf16[64,1024]{1,0:T(8,128)(2,1)S(1)}, bf16[64,1024]{1,0:T(8,128)(2,1)S(1)}, u32[]{:S(2)}, u32[]{:S(2)}) collective-permute-start(bf16[64,1024]{1,0:T(8,128)(2,1)S(1)} %select_select_fusion.refs_4_), channel_id=1, source_target_pairs={{0,64},{16,80},{32,96},{48,112},{64,0},{80,16},{96,32},{112,48},{1... | collective-permute-start | bytes 393224 | tf_op jit(solution)/shard_map/ppermute | solution.py:184
  49.0 25.3 %collective-permute-start.23 = (bf16[64,1024]{1,0:T(8,128)(2,1)S(1)}, bf16[64,1024]{1,0:T(8,128)(2,1)S(1)}, u32[]{:S(2)}, u32[]{:S(2)}) collective-permute-start(bf16[64,1024]{1,0:T(8,128)(2,1)S(1)} %select_select_fusion.refs_4_), channel_id=1, source_target_pairs={{0,96},{16,112},{32,0},{48,16},{64,32},{80,48},{96,64},{112,80},{1... | collective-permute-start | bytes 393224 | tf_op jit(solution)/shard_map/ppermute | solution.py:184
  69.9 6.3 %collective-permute-start.22 = (bf16[64,1024]{1,0:T(8,128)(2,1)S(1)}, bf16[64,1024]{1,0:T(8,128)(2,1)}, u32[]{:S(2)}, u32[]{:S(2)}) collective-permute-start(bf16[64,1024]{1,0:T(8,128)(2,1)S(1)} %select_select_fusion.refs_4_), channel_id=1, source_target_pairs={{0,32},{16,48},{32,64},{48,80},{64,96},{80,112},{96,0},{112,16},{1... | collective-permute-start | bytes 393224 | tf_op jit(solution)/shard_map/ppermute | solution.py:184
  71.8 44.6 %collective-permute-start.8 = (bf16[768,1024]{1,0:T(8,128)(2,1)}, bf16[768,1024]{1,0:T(8,128)(2,1)}, u32[]{:S(2)}, u32[]{:S(2)}) collective-permute-start(bf16[768,1024]{1,0:T(8,128)(2,1)} %constant_dynamic-update-slice_fusion), channel_id=1, source_target_pairs={{0,8},{1,9},{2,10},{3,11},{4,12},{5,13},{6,14},{7,15},{8,0},{9,1},... | collective-permute-start | bytes 4718600 | tf_op jit(solution)/shard_map/ppermute | solution.py:181
  71.8 44.6 %collective-permute-start.7 = (bf16[768,1024]{1,0:T(8,128)(2,1)}, bf16[768,1024]{1,0:T(8,128)(2,1)}, u32[]{:S(2)}, u32[]{:S(2)}) collective-permute-start(bf16[768,1024]{1,0:T(8,128)(2,1)} %constant_dynamic-update-slice_fusion), channel_id=1, source_target_pairs={{0,12},{1,13},{2,14},{3,15},{4,0},{5,1},{6,2},{7,3},{8,4},{9,5},{1... | collective-permute-start | bytes 4718600 | tf_op jit(solution)/shard_map/ppermute | solution.py:181
  74.9 41.5 %collective-permute-start.6 = (bf16[768,1024]{1,0:T(8,128)(2,1)}, bf16[768,1024]{1,0:T(8,128)(2,1)}, u32[]{:S(2)}, u32[]{:S(2)}) collective-permute-start(bf16[768,1024]{1,0:T(8,128)(2,1)} %constant_dynamic-update-slice_fusion), channel_id=1, source_target_pairs={{0,4},{1,5},{2,6},{3,7},{4,8},{5,9},{6,10},{7,11},{8,12},{9,13},{1... | collective-permute-start | bytes 4718600 | tf_op jit(solution)/shard_map/ppermute | solution.py:181
  77.5 11.3 %collective-permute-start.10 = (bf16[256,768]{1,0:T(8,128)(2,1)S(1)}, bf16[256,768]{1,0:T(8,128)(2,1)S(1)}, u32[]{:S(2)}, u32[]{:S(2)}) collective-permute-start(bf16[256,768]{1,0:T(8,128)(2,1)S(1)} %broadcast_select_fusion.refs_0_), channel_id=1, source_target_pairs={{0,32},{16,48},{32,0},{48,16},{64,96},{80,112},{96,64},{112,80},{1... | collective-permute-start | bytes 1179656 | tf_op jit(solution)/shard_map/ppermute | solution.py:184
  80.8 8.0 %collective-permute-start.11 = (bf16[256,768]{1,0:T(8,128)(2,1)S(1)}, bf16[256,768]{1,0:T(8,128)(2,1)S(1)}, u32[]{:S(2)}, u32[]{:S(2)}) collective-permute-start(bf16[256,768]{1,0:T(8,128)(2,1)S(1)} %broadcast_select_fusion.refs_0_), channel_id=1, source_target_pairs={{0,16},{16,0},{32,48},{48,32},{64,80},{80,64},{96,112},{112,96},{1... | collective-permute-start | bytes 1179656 | tf_op jit(solution)/shard_map/ppermute | solution.py:187
  88.9 27.3 %collective-permute-start.4 = (bf16[256,1024]{1,0:T(8,128)(2,1)}, bf16[256,1024]{1,0:T(8,128)(2,1)S(1)}, u32[]{:S(2)}, u32[]{:S(2)}) collective-permute-start(bf16[256,1024]{1,0:T(8,128)(2,1)} %refs_0_.1), channel_id=1, source_target_pairs={{0,12},{1,13},{2,14},{3,15},{4,0},{5,1},{6,2},{7,3},{8,4},{9,5},{1... | collective-permute-start | bytes 1572872 | tf_op jit(solution)/shard_map/ppermute | solution.py:181
  91.2 25.2 %collective-permute-start.3 = (bf16[256,1024]{1,0:T(8,128)(2,1)}, bf16[256,1024]{1,0:T(8,128)(2,1)S(1)}, u32[]{:S(2)}, u32[]{:S(2)}) collective-permute-start(bf16[256,1024]{1,0:T(8,128)(2,1)} %refs_0_.1), channel_id=1, source_target_pairs={{0,4},{1,5},{2,6},{3,7},{4,8},{5,9},{6,10},{7,11},{8,12},{9,13},{1... | collective-permute-start | bytes 1572872 | tf_op jit(solution)/shard_map/ppermute | solution.py:181
  (11 other events, 163.6 us)

commit v2 on v1

--- a/solution.py
+++ b/solution.py
@@ -1,3 +1,5 @@
+import functools
+
 import jax
 import jax.numpy as jnp
 from jax import lax
@@ -9,7 +11,9 @@
 BF = jnp.bfloat16
 F32 = jnp.float32
 SIDE = 4
-RING = 4
+RING = 3
+HALF = 128
+LIMIT = 28
 STEPS = (1, 3, 2)
 BOTH = ("row", "col")
 
@@ -41,63 +45,85 @@
     return jnp.dot(a, b, preferred_element_type=F32)
 
 
-def main_kernel(*refs):
-    own = refs[0]
-    near, turned, far = refs[1:4], refs[4:7], refs[7:10]
-    shared_ref, top_ref, rhs_ref, out_ref, obuf, osem = refs[10:]
-    size = own.shape[0]
+def update_kernel(tiles, first, *refs):
+    n_src = 1 + max(src for src, _, _ in tiles)
+    srcs = refs[:n_src]
+    shared_ref, top_ref, rhs_ref = refs[n_src : n_src + 3]
+    out_ref, obuf, osem, lbuf, lsem = refs[n_src + 3 + (not first) :]
+    size = top_ref.shape[0]
     row, col = lax.axis_index("row"), lax.axis_index("col")
     z, y = col // SIDE, col % SIDE
     core = lax.rem(row, 2)
 
-    def emit(slot, factor, along, across):
-        dy = jnp.where(core == 0, along, across)
-        dz = jnp.where(core == 0, across, along)
-        if slot >= RING:
-            pltpu.make_async_copy(obuf.at[0], obuf.at[0], osem.at[slot % RING]).wait()
-        slot = slot % RING
-        block = lax.rem(z + SIDE - dz, SIDE) * SIDE + lax.rem(y + SIDE - dy, SIDE)
-        begin = pl.multiple_of(block * size, size)
-        obuf[slot] = rhs_ref[pl.ds(begin, size), :].astype(F32) - dot(factor, shared_ref[...])
-
-        @pl.when(jnp.logical_and(block == 0, row < 4))
-        def _():
-            obuf[slot] = top_ref[...]
-
-        pltpu.make_async_copy(
-            obuf.at[slot], out_ref.at[pl.ds(begin, size), :], osem.at[slot]
-        ).start()
-
-    emit(0, own[...], 0, 0)
-    for i, d in enumerate(STEPS):
-        emit(1 + i, near[i][...], d, 0)
-        emit(4 + i, turned[i][...], 0, d)
-    for i, e in enumerate(STEPS):
-        for j, d in enumerate(STEPS):
-            emit(7 + 3 * i + j, far[i][j * size : (j + 1) * size, :], d, e)
-    for slot in range(RING):
-        pltpu.make_async_copy(obuf.at[slot], obuf.at[slot], osem.at[slot]).wait()
-
-
-def main_call(own, near, turned, far, shared, top, rhs):
+    def fetch(t):
+        src, start, pieces = tiles[t]
+        rows = sum(count for count, _, _, _ in pieces)
+        return pltpu.make_async_copy(
+            srcs[src].at[pl.ds(start, rows)], lbuf.at[t, pl.ds(0, rows)], lsem.at[t]
+        )
+
+    for t in range(len(tiles)):
+        fetch(t).start()
+
+    def finish(t):
+        rows = sum(count for count, _, _, _ in tiles[t][2])
+        part = obuf.at[t % RING, pl.ds(0, rows)]
+        pltpu.make_async_copy(part, part, osem.at[t % RING]).wait()
+
+    for t, (_, _, pieces) in enumerate(tiles):
+        if t >= RING:
+            finish(t - RING)
+        slot = t % RING
+        rows = sum(count for count, _, _, _ in pieces)
+        fetch(t).wait()
+        product = dot(lbuf[t, :rows, :], shared_ref[...])
+        at = 0
+        for count, along, across, offset in pieces:
+            dy = jnp.where(core == 0, along, across)
+            dz = jnp.where(core == 0, across, along)
+            block = lax.rem(z + SIDE - dz, SIDE) * SIDE + lax.rem(y + SIDE - dy, SIDE)
+            begin = pl.multiple_of(block * size + offset, HALF)
+            right = rhs_ref[pl.ds(begin, count), :].astype(F32)
+            obuf[slot, at : at + count, :] = right - product[at : at + count]
+
+            @pl.when(jnp.logical_and(block == 0, row < 4))
+            def _():
+                obuf[slot, at : at + count, :] = top_ref[offset : offset + count, :]
+
+            pltpu.make_async_copy(
+                obuf.at[slot, pl.ds(at, count)], out_ref.at[pl.ds(begin, count)], osem.at[slot]
+            ).start()
+            at += count
+    for t in range(max(0, len(tiles) - RING), len(tiles)):
+        finish(t)
+
+
+def update_call(srcs, tiles, shared, top, rhs, out):
     rows, width = rhs.shape
-    size, depth = own.shape
+    depth = shared.shape[0]
+    first = out is None
     vmem = pl.BlockSpec(memory_space=pltpu.VMEM)
-    args = [own, *near, *turned, *far, shared, top, rhs]
+    anywhere = pl.BlockSpec(memory_space=pl.ANY)
+    args = [*srcs, shared, top, rhs] + ([] if first else [out])
+    specs = [anywhere] * len(srcs) + [vmem] * 3 + ([] if first else [anywhere])
+    tallest = max(sum(p[0] for p in pieces) for _, _, pieces in tiles)
+    total = sum(p[0] for _, _, pieces in tiles for p in pieces)
     return pl.pallas_call(
-        main_kernel,
+        functools.partial(update_kernel, tiles, first),
         out_shape=jax.ShapeDtypeStruct((rows, width), F32),
-        in_specs=[vmem] * len(args),
-        out_specs=pl.BlockSpec(memory_space=pl.ANY),
+        in_specs=specs,
+        out_specs=anywhere,
+        input_output_aliases={} if first else {len(args) - 1: 0},
         scratch_shapes=[
-            pltpu.VMEM((RING, size, width), F32),
+            pltpu.VMEM((RING, tallest, width), F32),
             pltpu.SemaphoreType.DMA((RING,)),
+            pltpu.VMEM((len(tiles), tallest, depth), BF),
+            pltpu.SemaphoreType.DMA((len(tiles),)),
         ],
-        compiler_params=pltpu.CompilerParams(vmem_limit_bytes=24 << 20),
+        compiler_params=pltpu.CompilerParams(vmem_limit_bytes=LIMIT << 20),
         cost_estimate=pl.CostEstimate(
-            flops=2 * rows * depth * width, bytes_accessed=rows * width * 4, transcendentals=0
+            flops=2 * total * depth * width, bytes_accessed=total * width * 4, transcendentals=0
         ),
-        name="update",
     )(*args)
 
 
@@ -109,7 +135,13 @@
 def solve_kernel(*refs):
     own_rows, other_rows = refs[0:2], refs[2:4]
     own_low, other_low = refs[4:8], refs[8:12]
-    inverse_ref, shared_ref, top_ref, low = refs[12:]
+    inverse_hbm, shared_ref, top_ref, low, inverse_ref, sem = refs[12:]
+    copies = []
+    for k in range(inverse_hbm.shape[0]):
+        copies.append(
+            pltpu.make_async_copy(inverse_hbm.at[k], inverse_ref.at[k], sem.at[k])
+        )
+        copies[k].start()
     row = lax.axis_index("row")
     x, core = row // 2, lax.rem(row, 2)
     size = inverse_ref.shape[1]
@@ -128,9 +160,11 @@
         if k:
             begin = 0 if k < 2 else size
             current -= dot(low[k % 2, :, begin : begin + k * size], shared_ref[: k * size, :])
+        copies[k].wait()
         ih, il = split(inverse_ref[k])
         ch, cl = split(current)
-        solved = dot(ih, ch) + (dot(ih, cl) + dot(il, ch))
+        both = dot(jnp.concatenate([ih, il], 0), ch)
+        solved = both[:size] + (dot(ih, cl) + both[size:])
         shared_ref[k * size : (k + 1) * size, :] = solved.astype(BF)
 
         @pl.when(row == k)
@@ -149,15 +183,49 @@
             jax.ShapeDtypeStruct((panels * size, width), BF),
             jax.ShapeDtypeStruct((size, width), F32),
         ),
-        in_specs=[vmem] * len(args),
+        in_specs=[vmem] * (len(args) - 1) + [pl.BlockSpec(memory_space=pltpu.HBM)],
         out_specs=(vmem, vmem),
-        scratch_shapes=[pltpu.VMEM((2, size, 4 * size), BF)],
+        scratch_shapes=[
+            pltpu.VMEM((2, size, 4 * size), BF),
+            pltpu.VMEM((panels, size, size), F32),
+            pltpu.SemaphoreType.DMA((panels,)),
+        ],
         compiler_params=pltpu.CompilerParams(vmem_limit_bytes=12 << 20),
         cost_estimate=pl.CostEstimate(
             flops=2 * 18 * size * size * width, bytes_accessed=6 << 20, transcendentals=0
         ),
         name="solve",
     )(*args)
+
+
+def copy_kernel(n_src, moves, *refs):
+    outs, sem = refs[n_src:-1], refs[-1]
+    copies = [
+        pltpu.make_async_copy(
+            refs[src].at[pl.ds(start, rows)], outs[dst].at[pl.ds(to, rows)], sem.at[i]
+        )
+        for i, (src, start, rows, dst, to) in enumerate(moves)
+    ]
+    for copy in copies:
+        copy.start()
+    for copy in copies:
+        copy.wait()
+
+
+def copy_call(srcs, moves, out_rows):
+    width = srcs[0].shape[1]
+    count = len(out_rows)
+    return pl.pallas_call(
+        functools.partial(copy_kernel, len(srcs), moves),
+        out_shape=[jax.ShapeDtypeStruct((rows, width), BF) for rows in out_rows],
+        in_specs=[pl.BlockSpec(memory_space=pl.ANY)] * len(srcs),
+        out_specs=[pl.BlockSpec(memory_space=pltpu.VMEM)] * count,
+        scratch_shapes=[pltpu.SemaphoreType.DMA((len(moves),))],
+        compiler_params=pltpu.CompilerParams(vmem_limit_bytes=4 << 20),
+        cost_estimate=pl.CostEstimate(
+            flops=0, bytes_accessed=4 * sum(out_rows) * width, transcendentals=0
+        ),
+    )(*srcs)
 
 
 def pick(index, at0, at1, at2, at3):
@@ -213,13 +281,34 @@
     own_rows = [mine, theirs]
     other_rows = [swap(mine), swap(theirs)]
 
-    far = [across(jnp.concatenate(near, 0), e) for e in STEPS]
+    stack = jnp.concatenate(near, 0)
+    far = {e: across(stack, e) for e in (1, 3)}
+    part = 3 * HALF
+    moves = [(0, 0, part, 0, 0), (1, part, part, 1, 0)]
+    upper, lower = copy_call([far[1], far[3]], moves, [part, part])
+    beyond = [across(upper, 1), across(lower, 3)]
 
     own_low = [low] + [over_x(low, lambda s: (s + d) % SIDE) for d in STEPS]
     other_low = [swap(v) for v in own_low]
 
     shared, top = solve_call(own_rows, other_rows, own_low, other_low, inverse_blocks)
-    return main_call(factor_panels, near, turned, far, shared, top, right_sides)
+
+    def halves(e):
+        one, three, two = ((d, e) for d in STEPS)
+        return [
+            [(size, *one, 0), (HALF, *three, 0)],
+            [(HALF, *three, HALF), (size, *two, 0)],
+        ]
+
+    tiles = [(0, 0, [(size, 0, 0, 0)])]
+    tiles += [(1, i * 3 * HALF, p) for i, p in enumerate(halves(0))]
+    tiles += [(2 + i, 0, [(size, 0, d, 0)]) for i, d in enumerate(STEPS)]
+    tiles += [(5, i * part, p) for i, p in enumerate(halves(1))]
+    tiles += [(6, i * part, p) for i, p in enumerate(halves(3))]
+    srcs = [factor_panels, stack, *turned, far[1], far[3]]
+    out = update_call(srcs, tiles, shared, top, right_sides, None)
+    tiles = [(i, 0, p) for i, p in enumerate(halves(2))]
+    return update_call(beyond, tiles, shared, top, right_sides, out)
 
 
 def solution(mesh):

time: 134 us -> 105 us (0.78); the launches traced: 132 us -> 105 us
  starting transfers between devices: 52.9 us -> 40.9 us
  waiting for transfers between devices: 46.5 us -> 36.8 us
  local copies, waits for them, and re-layouts: 9.11 us -> 4.55 us
    ppermute x9 -> x10, waiting for transfers between devices: 23.7 us -> 4.05 us  [across(): return lax.ppermute(value, BOTH, plane_perm(d, 1))]
    ppermute x8, starting transfers between devices: 29.9 us -> 12.4 us  [over_x(): return lax.ppermute(value, 'row', x_perm(move))]
    ppermute x6, waiting for transfers between devices: 3.45 us -> 14.2 us  [along(): return lax.ppermute(value, BOTH, plane_perm(d, 0))]
    ppermute x9 -> x10, starting transfers between devices: 13.1 us -> 17.7 us  [across(): return lax.ppermute(value, BOTH, plane_perm(d, 1))]
    unnamed x14 -> x10, local copies, waits for them, and re-layouts: 4.45 us -> 1.69 us
    pallas_call x1 -> x3, Pallas kernels: 15.7 us -> 15 us  [the longest x2 13.6 us: update_call(): pl.pallas_call(functools.partial(update_kernel, tiles, first), out_shape=...]
  transfers between devices with their start and end apart: 29 -> 30, of which waited for: 13 -> 11; matrix products, arithmetic and copies ran while one was open for 5% -> 6% of each run, Pallas kernels for 4% -> 15%
where the time goes in v2:
time: 105 us
  starting transfers between devices  40.9 us (39%)
  waiting for transfers between devices  36.8 us (35%)
  Pallas kernels  19.2 us (18%)
  local copies, waits for them, and re-layouts  4.55 us (4%)
  other arithmetic  3 us (3%)
    ppermute x10, starting transfers between devices, across(): return lax.ppermute(value, BOTH, plane_perm(d, 1))  17.7 us
    ppermute x8, waiting for transfers between devices, over_x(): return lax.ppermute(value, 'row', x_perm(move))  16.6 us
    ppermute x6, waiting for transfers between devices, along(): return lax.ppermute(value, BOTH, plane_perm(d, 0))  14.2 us
    pallas_call x2, Pallas kernels, update_call(): pl.pallas_call(functools.partial(update_kernel, tiles, first), out_shape=...  13.6 us
    ppermute x8, starting transfers between devices, over_x(): return lax.ppermute(value, 'row', x_perm(move))  12.4 us
    ppermute x6, starting transfers between devices, along(): return lax.ppermute(value, BOTH, plane_perm(d, 0))  9.93 us
    pallas_call x1, Pallas kernels, solve_call(): pl.pallas_call(solve_kernel, out_shape=(jax.ShapeDtypeStruct((panels * si...  4.21 us
    ppermute x10, waiting for transfers between devices, across(): return lax.ppermute(value, BOTH, plane_perm(d, 1))  4.05 us
  transfers between devices with their start and end apart: 30, of which 11 were waited for; matrix products, arithmetic and copies ran while one was open for 6% of the time, Pallas kernels for 15%

profile of v2, /device:TPU:0, one launch (start us, length us, event | category | flops | bytes accessed | tf_op | source)
XLA Modules:
  0.0 104.8 jit_solution(545557710839370779)
XLA Ops:
  1.0 3.2 %collective-permute-start.12 = (bf16[64,768]{1,0:T(8,128)(2,1)S(1)}, bf16[64,768]{1,0:T(8,128)(2,1)S(1)}, u32[]{:S(2)}, u32[]{:S(2)}) collective-permute-start(bf16[64,768]{1,0:T(8,128)(2,1)S(1)} %get-tuple-element.13), channel_id=1, source_target_pairs={{0,64},{16,80},{32,96},{48,112},{64,0},{80,16},{96,32},{112,48},{1... | collective-permute-start | bytes 294920 | tf_op jit(solution)/shard_map/ppermute | solution.py:252
  6.3 3.2 %collective-permute-start.2 = (bf16[256,1024]{1,0:T(8,128)(2,1)}, bf16[256,1024]{1,0:T(8,128)(2,1)S(1)}, u32[]{:S(2)}, u32[]{:S(2)}) collective-permute-start(bf16[256,1024]{1,0:T(8,128)(2,1)} %refs_0_.1), channel_id=1, source_target_pairs={{0,2},{1,3},{2,0},{3,1},{4,6},{5,7},{6,4},{7,5},{8,10},{9,11},{10,... | collective-permute-start | bytes 1572872 | tf_op jit(solution)/shard_map/ppermute | solution.py:246
  13.3 4.1 %collective-permute-start.16 = (bf16[64,1024]{1,0:T(8,128)(2,1)S(1)}, bf16[64,1024]{1,0:T(8,128)(2,1)S(1)}, u32[]{:S(2)}, u32[]{:S(2)}) collective-permute-start(bf16[64,1024]{1,0:T(8,128)(2,1)S(1)} %pad_maximum_fusion), channel_id=1, source_target_pairs={{0,12},{1,13},{2,14},{3,15},{4,0},{5,1},{6,2},{7,3},{8,4},{9,5},{1... | collective-permute-start | bytes 393224 | tf_op jit(solution)/shard_map/ppermute | solution.py:249
  17.4 6.8 %collective-permute-done = bf16[256,1024]{1,0:T(8,128)(2,1)S(1)} collective-permute-done((bf16[256,1024]{1,0:T(8,128)(2,1)}, bf16[256,1024]{1,0:T(8,128)(2,1)S(1)}, u32[]{:S(2)}, u32[]{:S(2)}) %collective-permute-start) | collective-permute-done | bytes 524320 | tf_op jit(solution)/shard_map/ppermute | solution.py:246
  24.2 1.9 %collective-permute-start.14 = (bf16[64,1024]{1,0:T(8,128)(2,1)S(1)}, bf16[64,1024]{1,0:T(8,128)(2,1)S(1)}, u32[]{:S(2)}, u32[]{:S(2)}) collective-permute-start(bf16[64,1024]{1,0:T(8,128)(2,1)S(1)} %pad_maximum_fusion), channel_id=1, source_target_pairs={{0,4},{1,5},{2,6},{3,7},{4,8},{5,9},{6,10},{7,11},{8,12},{9,13},{1... | collective-permute-start | bytes 393224 | tf_op jit(solution)/shard_map/ppermute | solution.py:249
  28.6 3.5 %collective-permute-start.4 = (bf16[768,1024]{1,0:T(8,128)(2,1)}, bf16[768,1024]{1,0:T(8,128)(2,1)}, u32[]{:S(2)}, u32[]{:S(2)}) collective-permute-start(bf16[768,1024]{1,0:T(8,128)(2,1)} %constant_dynamic-update-slice_fusion.refs_1_), channel_id=1, source_target_pairs={{0,12},{1,13},{2,14},{3,15},{4,0},{5,1},{6,2},{7,3},{8,4},{9,5},{1... | collective-permute-start | bytes 4718600 | tf_op jit(solution)/shard_map/ppermute | solution.py:249
  32.6 1.9 %collective-permute-start.19 = (bf16[64,1024]{1,0:T(8,128)(2,1)S(1)}, bf16[64,1024]{1,0:T(8,128)(2,1)S(1)}, u32[]{:S(2)}, u32[]{:S(2)}) collective-permute-start(bf16[64,1024]{1,0:T(8,128)(2,1)S(1)} %select_select_fusion.1), channel_id=1, source_target_pairs={{0,3},{1,0},{2,1},{3,2},{4,7},{5,4},{6,5},{7,6},{8,11},{9,8},{10,9... | collective-permute-start | bytes 393224 | tf_op jit(solution)/shard_map/ppermute | solution.py:246
  35.5 2.4 %collective-permute-start.7 = (bf16[256,768]{1,0:T(8,128)(2,1)S(1)}, bf16[256,768]{1,0:T(8,128)(2,1)}, u32[]{:S(2)}, u32[]{:S(2)}) collective-permute-start(bf16[256,768]{1,0:T(8,128)(2,1)S(1)} %slice.6), channel_id=1, source_target_pairs={{0,96},{16,112},{32,64},{48,80},{64,32},{80,48},{96,0},{112,16},{1... | collective-permute-start | bytes 1179656 | tf_op jit(solution)/shard_map/ppermute | solution.py:252
  37.9 2.0 %collective-permute-start.18 = (bf16[64,1024]{1,0:T(8,128)(2,1)S(1)}, bf16[64,1024]{1,0:T(8,128)(2,1)S(1)}, u32[]{:S(2)}, u32[]{:S(2)}) collective-permute-start(bf16[64,1024]{1,0:T(8,128)(2,1)S(1)} %select_select_fusion.1), channel_id=1, source_target_pairs={{0,2},{1,3},{2,0},{3,1},{4,6},{5,7},{6,4},{7,5},{8,10},{9,11},{10,... | collective-permute-start | bytes 393224 | tf_op jit(solution)/shard_map/ppermute | solution.py:246
  40.8 5.0 %collective-permute-done.18 = bf16[64,1024]{1,0:T(8,128)(2,1)S(1)} collective-permute-done((bf16[64,1024]{1,0:T(8,128)(2,1)S(1)}, bf16[64,1024]{1,0:T(8,128)(2,1)S(1)}, u32[]{:S(2)}, u32[]{:S(2)}) %collective-permute-start.18) | collective-permute-done | bytes 131104 | tf_op jit(solution)/shard_map/ppermute | solution.py:246
  45.8 2.4 %collective-permute-done.17 = bf16[64,1024]{1,0:T(8,128)(2,1)} collective-permute-done((bf16[64,1024]{1,0:T(8,128)(2,1)S(1)}, bf16[64,1024]{1,0:T(8,128)(2,1)}, u32[]{:S(2)}, u32[]{:S(2)}) %collective-permute-start.17) | collective-permute-done | bytes 131104 | tf_op jit(solution)/shard_map/ppermute | solution.py:246
  49.6 2.7 %collective-permute-start.22 = (bf16[64,1024]{1,0:T(8,128)(2,1)S(1)}, bf16[64,1024]{1,0:T(8,128)(2,1)S(1)}, u32[]{:S(2)}, u32[]{:S(2)}) collective-permute-start(bf16[64,1024]{1,0:T(8,128)(2,1)S(1)} %select_select_fusion.refs_4_), channel_id=1, source_target_pairs={{0,64},{16,80},{32,96},{48,112},{64,0},{80,16},{96,32},{112,48},{1... | collective-permute-start | bytes 393224 | tf_op jit(solution)/shard_map/ppermute | solution.py:252
  52.3 1.9 %collective-permute-start.21 = (bf16[64,1024]{1,0:T(8,128)(2,1)S(1)}, bf16[64,1024]{1,0:T(8,128)(2,1)S(1)}, u32[]{:S(2)}, u32[]{:S(2)}) collective-permute-start(bf16[64,1024]{1,0:T(8,128)(2,1)S(1)} %select_select_fusion.refs_4_), channel_id=1, source_target_pairs={{0,96},{16,112},{32,0},{48,16},{64,32},{80,48},{96,64},{112,80},{1... | collective-permute-start | bytes 393224 | tf_op jit(solution)/shard_map/ppermute | solution.py:252
  54.3 10.3 %collective-permute-done.22.refs_7_ = bf16[64,1024]{1,0:T(8,128)(2,1)S(1)} collective-permute-done((bf16[64,1024]{1,0:T(8,128)(2,1)S(1)}, bf16[64,1024]{1,0:T(8,128)(2,1)S(1)}, u32[]{:S(2)}, u32[]{:S(2)}) %collective-permute-start.22) | collective-permute-done | bytes 131104 | tf_op jit(solution)/shard_map/ppermute | solution.py:252
  64.6 2.1 %collective-permute-done.21.refs_6_ = bf16[64,1024]{1,0:T(8,128)(2,1)S(1)} collective-permute-done((bf16[64,1024]{1,0:T(8,128)(2,1)S(1)}, bf16[64,1024]{1,0:T(8,128)(2,1)S(1)}, u32[]{:S(2)}, u32[]{:S(2)}) %collective-permute-start.21) | collective-permute-done | bytes 131104 | tf_op jit(solution)/shard_map/ppermute | solution.py:252
  66.7 4.1 %collective-permute-done.20.refs_5_ = bf16[64,1024]{1,0:T(8,128)(2,1)S(1)} collective-permute-done((bf16[64,1024]{1,0:T(8,128)(2,1)S(1)}, bf16[64,1024]{1,0:T(8,128)(2,1)S(1)}, u32[]{:S(2)}, u32[]{:S(2)}) %collective-permute-start.20) | collective-permute-done | bytes 131104 | tf_op jit(solution)/shard_map/ppermute | solution.py:252
  74.3 2.5 %collective-permute-start.28 = (bf16[256,1024]{1,0:T(8,128)(2,1)S(1)}, bf16[256,1024]{1,0:T(8,128)(2,1)S(1)}, u32[]{:S(2)}, u32[]{:S(2)}) collective-permute-start(bf16[256,1024]{1,0:T(8,128)(2,1)S(1)} %copy-done), channel_id=1, source_target_pairs={{0,12},{1,13},{2,14},{3,15},{4,0},{5,1},{6,2},{7,3},{8,4},{9,5},{1... | collective-permute-start | bytes 1572872 | tf_op jit(solution)/shard_map/ppermute | solution.py:249
  76.8 1.6 %collective-permute-start.29 = (bf16[256,1024]{1,0:T(8,128)(2,1)S(1)}, bf16[256,1024]{1,0:T(8,128)(2,1)S(1)}, u32[]{:S(2)}, u32[]{:S(2)}) collective-permute-start(bf16[256,1024]{1,0:T(8,128)(2,1)S(1)} %copy-done), channel_id=1, source_target_pairs={{0,8},{1,9},{2,10},{3,11},{4,12},{5,13},{6,14},{7,15},{8,0},{9,1},... | collective-permute-start | bytes 1572872 | tf_op jit(solution)/shard_map/ppermute | solution.py:249
  81.0 2.1 %collective-permute-start.6 = (bf16[384,1024]{1,0:T(8,128)(2,1)S(1)}, bf16[384,1024]{1,0:T(8,128)(2,1)S(1)}, u32[]{:S(2)}, u32[]{:S(2)}) collective-permute-start(bf16[384,1024]{1,0:T(8,128)(2,1)S(1)} %get-tuple-element.10), channel_id=1, source_target_pairs={{0,12},{1,13},{2,14},{3,15},{4,0},{5,1},{6,2},{7,3},{8,4},{9,5},{1... | collective-permute-start | bytes 2359304 | tf_op jit(solution)/shard_map/ppermute | solution.py:249
  83.1 4.2 %solve.1 = (bf16[1024,768]{1,0:T(8,128)(2,1)S(1)}, f32[256,768]{1,0:T(8,128)S(1)}) custom-call(bf16[256,768]{1,0:T(8,128)(2,1)S(1)} %broadcast_select_fusion.refs_0_, bf16[256,768]{1,0:T(8,128)(2,1)S(1)} %collective-permute-done.8.refs_1_, bf16[256,768]{1,0:T(8,128)(2,1)S(1)} %collective-permute-done.9.refs_2_, ...), custom_call_target="tpu_custom_call" | custom-call | flops 1811939328 | bytes 6291456 | tf_op jit(solution)/shard_map/solve/pallas_call | solution.py:180
  87.3 1.8 %collective-permute-done.28.refs_3_ = bf16[256,1024]{1,0:T(8,128)(2,1)S(1)} collective-permute-done((bf16[256,1024]{1,0:T(8,128)(2,1)S(1)}, bf16[256,1024]{1,0:T(8,128)(2,1)S(1)}, u32[]{:S(2)}, u32[]{:S(2)}) %collective-permute-start.28) | collective-permute-done | bytes 524320 | tf_op jit(solution)/shard_map/ppermute | solution.py:249
  89.1 1.8 %collective-permute-done.29.refs_4_ = bf16[256,1024]{1,0:T(8,128)(2,1)S(1)} collective-permute-done((bf16[256,1024]{1,0:T(8,128)(2,1)S(1)}, bf16[256,1024]{1,0:T(8,128)(2,1)S(1)}, u32[]{:S(2)}, u32[]{:S(2)}) %collective-permute-start.29) | collective-permute-done | bytes 524320 | tf_op jit(solution)/shard_map/ppermute | solution.py:249
  91.0 10.5 %shard_map.38.refs_5_ = f32[4096,768]{1,0:T(8,128)} custom-call(bf16[256,1024]{1,0:T(8,128)(2,1)S(1)} %copy-done, bf16[768,1024]{1,0:T(8,128)(2,1)} %constant_dynamic-update-slice_fusion.refs_1_, bf16[256,1024]{1,0:T(8,128)(2,1)S(1)} %collective-permute-done.27.refs_2_, bf16[256,1024]{1,0:T(8,128)(2,1)S(1)} %collective-permute-done.28.refs_3_, ...), custom_call_target="tpu_custom_call" | custom-call | flops 5234491392 | bytes 10223616 | tf_op jit(solution)/shard_map/pallas_call | solution.py:111
  101.5 3.2 %shard_map.39 = f32[4096,768]{1,0:T(8,128)} custom-call(bf16[384,1024]{1,0:T(8,128)(2,1)S(1)} %collective-permute-done.5.refs_0_, bf16[384,1024]{1,0:T(8,128)(2,1)S(1)} %collective-permute-done.6.refs_1_, bf16[1024,768]{1,0:T(8,128)(2,1)S(1)} %get-tuple-element.11.refs_7_.refs_2_, ...), custom_call_target="tpu_custom_call", output_to_operand_aliasing={{}: (5, {})} | custom-call | flops 1207959552 | bytes 2359296 | tf_op jit(solution)/shard_map/pallas_call | solution.py:111
  (60 shorter events, 19.1 us)
Async XLA Ops:
  1.0 9.5 %collective-permute-start.12 = (bf16[64,768]{1,0:T(8,128)(2,1)S(1)}, bf16[64,768]{1,0:T(8,128)(2,1)S(1)}, u32[]{:S(2)}, u32[]{:S(2)}) collective-permute-start(bf16[64,768]{1,0:T(8,128)(2,1)S(1)} %get-tuple-element.13), channel_id=1, source_target_pairs={{0,64},{16,80},{32,96},{48,112},{64,0},{80,16},{96,32},{112,48},{1... | collective-permute-start | bytes 294920 | tf_op jit(solution)/shard_map/ppermute | solution.py:252
  4.2 7.3 %collective-permute-start.13 = (bf16[64,768]{1,0:T(8,128)(2,1)S(1)}, bf16[64,768]{1,0:T(8,128)(2,1)S(1)}, u32[]{:S(2)}, u32[]{:S(2)}) collective-permute-start(bf16[64,768]{1,0:T(8,128)(2,1)S(1)} %get-tuple-element.14), channel_id=1, source_target_pairs={{0,96},{16,112},{32,0},{48,16},{64,32},{80,48},{96,64},{112,80},{1... | collective-permute-start | bytes 294920 | tf_op jit(solution)/shard_map/ppermute | solution.py:252
  6.3 21.5 %collective-permute-start.2 = (bf16[256,1024]{1,0:T(8,128)(2,1)}, bf16[256,1024]{1,0:T(8,128)(2,1)S(1)}, u32[]{:S(2)}, u32[]{:S(2)}) collective-permute-start(bf16[256,1024]{1,0:T(8,128)(2,1)} %refs_0_.1), channel_id=1, source_target_pairs={{0,2},{1,3},{2,0},{3,1},{4,6},{5,7},{6,4},{7,5},{8,10},{9,11},{10,... | collective-permute-start | bytes 1572872 | tf_op jit(solution)/shard_map/ppermute | solution.py:246
  9.4 17.5 %collective-permute-start.1 = (bf16[256,1024]{1,0:T(8,128)(2,1)}, bf16[256,1024]{1,0:T(8,128)(2,1)S(1)}, u32[]{:S(2)}, u32[]{:S(2)}) collective-permute-start(bf16[256,1024]{1,0:T(8,128)(2,1)} %refs_0_.1), channel_id=1, source_target_pairs={{0,3},{1,0},{2,1},{3,2},{4,7},{5,4},{6,5},{7,6},{8,11},{9,8},{10,9... | collective-permute-start | bytes 1572872 | tf_op jit(solution)/shard_map/ppermute | solution.py:246
  10.5 13.7 %collective-permute-start = (bf16[256,1024]{1,0:T(8,128)(2,1)}, bf16[256,1024]{1,0:T(8,128)(2,1)S(1)}, u32[]{:S(2)}, u32[]{:S(2)}) collective-permute-start(bf16[256,1024]{1,0:T(8,128)(2,1)} %refs_0_.1), channel_id=1, source_target_pairs={{0,1},{1,2},{2,3},{3,0},{4,5},{5,6},{6,7},{7,4},{8,9},{9,10},{10,1... | collective-permute-start | bytes 1572872 | tf_op jit(solution)/shard_map/ppermute | solution.py:246
  13.3 18.9 %collective-permute-start.16 = (bf16[64,1024]{1,0:T(8,128)(2,1)S(1)}, bf16[64,1024]{1,0:T(8,128)(2,1)S(1)}, u32[]{:S(2)}, u32[]{:S(2)}) collective-permute-start(bf16[64,1024]{1,0:T(8,128)(2,1)S(1)} %pad_maximum_fusion), channel_id=1, source_target_pairs={{0,12},{1,13},{2,14},{3,15},{4,0},{5,1},{6,2},{7,3},{8,4},{9,5},{1... | collective-permute-start | bytes 393224 | tf_op jit(solution)/shard_map/ppermute | solution.py:249
  17.4 14.8 %collective-permute-start.15 = (bf16[64,1024]{1,0:T(8,128)(2,1)S(1)}, bf16[64,1024]{1,0:T(8,128)(2,1)S(1)}, u32[]{:S(2)}, u32[]{:S(2)}) collective-permute-start(bf16[64,1024]{1,0:T(8,128)(2,1)S(1)} %pad_maximum_fusion), channel_id=1, source_target_pairs={{0,8},{1,9},{2,10},{3,11},{4,12},{5,13},{6,14},{7,15},{8,0},{9,1},... | collective-permute-start | bytes 393224 | tf_op jit(solution)/shard_map/ppermute | solution.py:249
  24.2 8.4 %collective-permute-start.14 = (bf16[64,1024]{1,0:T(8,128)(2,1)S(1)}, bf16[64,1024]{1,0:T(8,128)(2,1)S(1)}, u32[]{:S(2)}, u32[]{:S(2)}) collective-permute-start(bf16[64,1024]{1,0:T(8,128)(2,1)S(1)} %pad_maximum_fusion), channel_id=1, source_target_pairs={{0,4},{1,5},{2,6},{3,7},{4,8},{5,9},{6,10},{7,11},{8,12},{9,13},{1... | collective-permute-start | bytes 393224 | tf_op jit(solution)/shard_map/ppermute | solution.py:249
  28.6 45.7 %collective-permute-start.4 = (bf16[768,1024]{1,0:T(8,128)(2,1)}, bf16[768,1024]{1,0:T(8,128)(2,1)}, u32[]{:S(2)}, u32[]{:S(2)}) collective-permute-start(bf16[768,1024]{1,0:T(8,128)(2,1)} %constant_dynamic-update-slice_fusion.refs_1_), channel_id=1, source_target_pairs={{0,12},{1,13},{2,14},{3,15},{4,0},{5,1},{6,2},{7,3},{8,4},{9,5},{1... | collective-permute-start | bytes 4718600 | tf_op jit(solution)/shard_map/ppermute | solution.py:249
  32.1 44.6 %collective-permute-start.3 = (bf16[768,1024]{1,0:T(8,128)(2,1)}, bf16[768,1024]{1,0:T(8,128)(2,1)}, u32[]{:S(2)}, u32[]{:S(2)}) collective-permute-start(bf16[768,1024]{1,0:T(8,128)(2,1)} %constant_dynamic-update-slice_fusion.refs_1_), channel_id=1, source_target_pairs={{0,4},{1,5},{2,6},{3,7},{4,8},{5,9},{6,10},{7,11},{8,12},{9,13},{1... | collective-permute-start | bytes 4718600 | tf_op jit(solution)/shard_map/ppermute | solution.py:249
  32.6 7.3 %collective-permute-start.19 = (bf16[64,1024]{1,0:T(8,128)(2,1)S(1)}, bf16[64,1024]{1,0:T(8,128)(2,1)S(1)}, u32[]{:S(2)}, u32[]{:S(2)}) collective-permute-start(bf16[64,1024]{1,0:T(8,128)(2,1)S(1)} %select_select_fusion.1), channel_id=1, source_target_pairs={{0,3},{1,0},{2,1},{3,2},{4,7},{5,4},{6,5},{7,6},{8,11},{9,8},{10,9... | collective-permute-start | bytes 393224 | tf_op jit(solution)/shard_map/ppermute | solution.py:246
  35.5 12.8 %collective-permute-start.7 = (bf16[256,768]{1,0:T(8,128)(2,1)S(1)}, bf16[256,768]{1,0:T(8,128)(2,1)}, u32[]{:S(2)}, u32[]{:S(2)}) collective-permute-start(bf16[256,768]{1,0:T(8,128)(2,1)S(1)} %slice.6), channel_id=1, source_target_pairs={{0,96},{16,112},{32,64},{48,80},{64,32},{80,48},{96,0},{112,16},{1... | collective-permute-start | bytes 1179656 | tf_op jit(solution)/shard_map/ppermute | solution.py:252
  37.9 7.9 %collective-permute-start.18 = (bf16[64,1024]{1,0:T(8,128)(2,1)S(1)}, bf16[64,1024]{1,0:T(8,128)(2,1)S(1)}, u32[]{:S(2)}, u32[]{:S(2)}) collective-permute-start(bf16[64,1024]{1,0:T(8,128)(2,1)S(1)} %select_select_fusion.1), channel_id=1, source_target_pairs={{0,2},{1,3},{2,0},{3,1},{4,6},{5,7},{6,4},{7,5},{8,10},{9,11},{10,... | collective-permute-start | bytes 393224 | tf_op jit(solution)/shard_map/ppermute | solution.py:246
  40.0 8.2 %collective-permute-start.17 = (bf16[64,1024]{1,0:T(8,128)(2,1)S(1)}, bf16[64,1024]{1,0:T(8,128)(2,1)}, u32[]{:S(2)}, u32[]{:S(2)}) collective-permute-start(bf16[64,1024]{1,0:T(8,128)(2,1)S(1)} %select_select_fusion.1), channel_id=1, source_target_pairs={{0,1},{1,2},{2,3},{3,0},{4,5},{5,6},{6,7},{7,4},{8,9},{9,10},{10,1... | collective-permute-start | bytes 393224 | tf_op jit(solution)/shard_map/ppermute | solution.py:246
  49.5 21.9 %collective-permute-start.8 = (bf16[256,768]{1,0:T(8,128)(2,1)S(1)}, bf16[256,768]{1,0:T(8,128)(2,1)S(1)}, u32[]{:S(2)}, u32[]{:S(2)}) collective-permute-start(bf16[256,768]{1,0:T(8,128)(2,1)S(1)} %broadcast_select_fusion.refs_0_), channel_id=1, source_target_pairs={{0,32},{16,48},{32,0},{48,16},{64,96},{80,112},{96,64},{112,80},{1... | collective-permute-start | bytes 1179656 | tf_op jit(solution)/shard_map/ppermute | solution.py:252
  49.6 15.0 %collective-permute-start.22 = (bf16[64,1024]{1,0:T(8,128)(2,1)S(1)}, bf16[64,1024]{1,0:T(8,128)(2,1)S(1)}, u32[]{:S(2)}, u32[]{:S(2)}) collective-permute-start(bf16[64,1024]{1,0:T(8,128)(2,1)S(1)} %select_select_fusion.refs_4_), channel_id=1, source_target_pairs={{0,64},{16,80},{32,96},{48,112},{64,0},{80,16},{96,32},{112,48},{1... | collective-permute-start | bytes 393224 | tf_op jit(solution)/shard_map/ppermute | solution.py:252
  52.3 14.4 %collective-permute-start.21 = (bf16[64,1024]{1,0:T(8,128)(2,1)S(1)}, bf16[64,1024]{1,0:T(8,128)(2,1)S(1)}, u32[]{:S(2)}, u32[]{:S(2)}) collective-permute-start(bf16[64,1024]{1,0:T(8,128)(2,1)S(1)} %select_select_fusion.refs_4_), channel_id=1, source_target_pairs={{0,96},{16,112},{32,0},{48,16},{64,32},{80,48},{96,64},{112,80},{1... | collective-permute-start | bytes 393224 | tf_op jit(solution)/shard_map/ppermute | solution.py:252
  70.8 9.0 %collective-permute-start.9 = (bf16[256,768]{1,0:T(8,128)(2,1)S(1)}, bf16[256,768]{1,0:T(8,128)(2,1)S(1)}, u32[]{:S(2)}, u32[]{:S(2)}) collective-permute-start(bf16[256,768]{1,0:T(8,128)(2,1)S(1)} %broadcast_select_fusion.refs_0_), channel_id=1, source_target_pairs={{0,16},{16,0},{32,48},{48,32},{64,80},{80,64},{96,112},{112,96},{1... | collective-permute-start | bytes 1179656 | tf_op jit(solution)/shard_map/ppermute | solution.py:255
  71.3 9.7 %collective-permute-start.10 = (bf16[256,768]{1,0:T(8,128)(2,1)S(1)}, bf16[256,768]{1,0:T(8,128)(2,1)S(1)}, u32[]{:S(2)}, u32[]{:S(2)}) collective-permute-start(bf16[256,768]{1,0:T(8,128)(2,1)S(1)} %collective-permute-done.8.refs_1_), channel_id=1, source_target_pairs={{0,16},{16,0},{32,48},{48,32},{64,80},{80,64},{96,112},{112,96},{1... | collective-permute-start | bytes 1179656 | tf_op jit(solution)/shard_map/ppermute | solution.py:255
  73.5 13.8 %collective-permute-start.27 = (bf16[256,1024]{1,0:T(8,128)(2,1)S(1)}, bf16[256,1024]{1,0:T(8,128)(2,1)S(1)}, u32[]{:S(2)}, u32[]{:S(2)}) collective-permute-start(bf16[256,1024]{1,0:T(8,128)(2,1)S(1)} %copy-done), channel_id=1, source_target_pairs={{0,4},{1,5},{2,6},{3,7},{4,8},{5,9},{6,10},{7,11},{8,12},{9,13},{1... | collective-permute-start | bytes 1572872 | tf_op jit(solution)/shard_map/ppermute | solution.py:249
  74.3 14.8 %collective-permute-start.28 = (bf16[256,1024]{1,0:T(8,128)(2,1)S(1)}, bf16[256,1024]{1,0:T(8,128)(2,1)S(1)}, u32[]{:S(2)}, u32[]{:S(2)}) collective-permute-start(bf16[256,1024]{1,0:T(8,128)(2,1)S(1)} %copy-done), channel_id=1, source_target_pairs={{0,12},{1,13},{2,14},{3,15},{4,0},{5,1},{6,2},{7,3},{8,4},{9,5},{1... | collective-permute-start | bytes 1572872 | tf_op jit(solution)/shard_map/ppermute | solution.py:249
  76.8 14.2 %collective-permute-start.29 = (bf16[256,1024]{1,0:T(8,128)(2,1)S(1)}, bf16[256,1024]{1,0:T(8,128)(2,1)S(1)}, u32[]{:S(2)}, u32[]{:S(2)}) collective-permute-start(bf16[256,1024]{1,0:T(8,128)(2,1)S(1)} %copy-done), channel_id=1, source_target_pairs={{0,8},{1,9},{2,10},{3,11},{4,12},{5,13},{6,14},{7,15},{8,0},{9,1},... | collective-permute-start | bytes 1572872 | tf_op jit(solution)/shard_map/ppermute | solution.py:249
  79.8 21.7 %collective-permute-start.5 = (bf16[384,1024]{1,0:T(8,128)(2,1)S(1)}, bf16[384,1024]{1,0:T(8,128)(2,1)S(1)}, u32[]{:S(2)}, u32[]{:S(2)}) collective-permute-start(bf16[384,1024]{1,0:T(8,128)(2,1)S(1)} %get-tuple-element.9), channel_id=1, source_target_pairs={{0,4},{1,5},{2,6},{3,7},{4,8},{5,9},{6,10},{7,11},{8,12},{9,13},{1... | collective-permute-start | bytes 2359304 | tf_op jit(solution)/shard_map/ppermute | solution.py:249
  81.0 20.5 %collective-permute-start.6 = (bf16[384,1024]{1,0:T(8,128)(2,1)S(1)}, bf16[384,1024]{1,0:T(8,128)(2,1)S(1)}, u32[]{:S(2)}, u32[]{:S(2)}) collective-permute-start(bf16[384,1024]{1,0:T(8,128)(2,1)S(1)} %get-tuple-element.10), channel_id=1, source_target_pairs={{0,12},{1,13},{2,14},{3,15},{4,0},{5,1},{6,2},{7,3},{8,4},{9,5},{1... | collective-permute-start | bytes 2359304 | tf_op jit(solution)/shard_map/ppermute | solution.py:249
  (10 other events, 204.2 us)
